TPU v7x, 32 devices: a whole 2x2x4 slice. The times are simulated.
32 devices in a mesh: fsdp: 2 (over core), ctx: 4 (over y, x), tp: 4 (over z).
Axes of the slice: x: 2, y: 2, z: 4, core: 2. Of those that a mesh axis runs over, the one named last changes fastest.
Arguments:
- x_prompt: bfloat16 [2, 1024, 1024], P('fsdp', 'ctx'), may hold values from -6 to 6
- x_cont: bfloat16 [2, 12, 256, 1024], P('fsdp', 'ctx'), may hold values from -6 to 6
- cont_start: int32 [2, 12], P('fsdp', 'ctx'), may hold values from 512 to 1024
- w_qkv: bfloat16 [1024, 3, 1024], P(('fsdp', 'ctx'), None, 'tp'), may hold values from -0.1875 to 0.1875
- qkv_bias: bfloat16 [3, 1024], P(None, 'tp'), may hold values from -3 to 3
- w_dense: bfloat16 [1024, 1024], P('tp', ('fsdp', 'ctx')), may hold values from -0.75 to 0.75
- dense_bias: bfloat16 [1024], P(('fsdp', 'ctx')), may hold values from -3 to 3
- w_fc1: bfloat16 [1024, 4096], P(('fsdp', 'ctx'), 'tp'), may hold values from -0.1875 to 0.1875
- fc1_bias: bfloat16 [4096], P('tp'), may hold values from -3 to 3
- w_fc2: bfloat16 [4096, 1024], P('tp', ('fsdp', 'ctx')), may hold values from -0.09375 to 0.09375
- fc2_bias: bfloat16 [1024], P(('fsdp', 'ctx')), may hold values from -3 to 3
- ln1_gain: bfloat16 [1024], P(('fsdp', 'ctx')), may hold values from 0.099609375 to 1.8984375
- ln1_bias: bfloat16 [1024], P(('fsdp', 'ctx')), may hold values from -2 to 2
- ln2_gain: bfloat16 [1024], P(('fsdp', 'ctx')), may hold values from 0.099609375 to 1.8984375
- ln2_bias: bfloat16 [1024], P(('fsdp', 'ctx')), may hold values from -2 to 2
- dy_prompt: bfloat16 [2, 1024, 1024], P('fsdp', 'ctx'), may hold values from -6 to 6
- dy_cont: bfloat16 [2, 12, 256, 1024], P('fsdp', 'ctx'), may hold values from -6 to 6
Outputs:
- y_prompt: float32 [2, 1024, 1024], P('fsdp', 'ctx')
- y_cont: float32 [2, 12, 256, 1024], P('fsdp', 'ctx')
- dx_prompt: float32 [2, 1024, 1024], P('fsdp', 'ctx')
- dx_cont: float32 [2, 12, 256, 1024], P('fsdp', 'ctx')
- d_w_qkv: float32 [1024, 3, 1024], P(('fsdp', 'ctx'), None, 'tp')
- d_qkv_bias: float32 [3, 1024], P(None, 'tp')
- d_w_dense: float32 [1024, 1024], P('tp', ('fsdp', 'ctx'))
- d_dense_bias: float32 [1024], P(('fsdp', 'ctx'))
- d_w_fc1: float32 [1024, 4096], P(('fsdp', 'ctx'), 'tp')
- d_fc1_bias: float32 [4096], P('tp')
- d_w_fc2: float32 [4096, 1024], P('tp', ('fsdp', 'ctx'))
- d_fc2_bias: float32 [1024], P(('fsdp', 'ctx'))
- d_ln1_gain: float32 [1024], P(('fsdp', 'ctx'))
- d_ln1_bias: float32 [1024], P(('fsdp', 'ctx'))
- d_ln2_gain: float32 [1024], P(('fsdp', 'ctx'))
- d_ln2_bias: float32 [1024], P(('fsdp', 'ctx'))
Inputs may be any that keep to these rules, and one draw needn't show every extreme that they name: `cont_start`: a continuation follows the prompt tokens before its first position.
All inputs are finite; a program needn't handle non-finite values.
Results may differ from a plain program's by a relative error of at most 0.012.
Values may be sent and summed in bfloat16 or wider, within the bound.
A program may use at most 192 MiB of HBM per device.

v0:
```python
import jax
import jax.numpy as jnp
from jax import lax
from jax.sharding import PartitionSpec as P

HD = 64
ROT = 16
EPS = 1e-05


def exact_gelu(values):
    return jax.nn.gelu(values, approximate=False)


def rotary_tables(positions):
    freq_index = jnp.arange(ROT // 2).astype(jnp.float32)
    inverse = jnp.power(10000.0, -2.0 * freq_index / ROT)
    phase = positions.astype(jnp.float32)[..., None] * inverse
    cos_half = jnp.cos(phase)
    sin_half = jnp.sin(phase)
    return (
        jnp.concatenate([cos_half, cos_half], axis=-1),
        jnp.concatenate([sin_half, sin_half], axis=-1),
    )


def rotate(inputs, cos_t, sin_t):
    leading = inputs[..., :ROT]
    half_rot = ROT // 2
    turned = jnp.concatenate([-leading[..., half_rot:], leading[..., :half_rot]], axis=-1)
    return jnp.concatenate([leading * cos_t + turned * sin_t, inputs[..., ROT:]], axis=-1)


def masked_scores(
    queries, all_keys, key_limit, query_slot, query_offs, prompt_len, key_slot, key_offs
):
    raw_scores = jnp.einsum("qhd,khd->hqk", queries, all_keys, preferred_element_type=jnp.float32)
    key_index = jnp.arange(all_keys.shape[0], dtype=jnp.int32)
    near_keys = key_index[None, :] < key_limit[:, None]
    own_keys = (key_slot[None, :] == query_slot[:, None]) & (
        key_offs[None, :] <= query_offs[:, None]
    )
    allowed = jnp.where((key_index < prompt_len)[None, :], near_keys, own_keys)
    return jnp.where(allowed[None], raw_scores * 0.125, -1e30)


def on_device(
    x_prompt,
    x_cont,
    cont_start,
    w_qkv,
    qkv_bias,
    w_dense,
    dense_bias,
    w_fc1,
    fc1_bias,
    w_fc2,
    fc2_bias,
    ln1_gain,
    ln1_bias,
    ln2_gain,
    ln2_bias,
    dy_prompt,
    dy_cont,
):
    gathered = (
        lax.all_gather(w_qkv, ("fsdp", "ctx"), axis=0, tiled=True),
        lax.all_gather(w_dense, ("fsdp", "ctx"), axis=1, tiled=True),
        lax.all_gather(w_fc1, ("fsdp", "ctx"), axis=0, tiled=True),
        lax.all_gather(w_fc2, ("fsdp", "ctx"), axis=1, tiled=True),
        lax.all_gather(dense_bias, ("fsdp", "ctx"), axis=0, tiled=True),
        lax.all_gather(fc2_bias, ("fsdp", "ctx"), axis=0, tiled=True),
        lax.all_gather(ln1_gain, ("fsdp", "ctx"), axis=0, tiled=True),
        lax.all_gather(ln1_bias, ("fsdp", "ctx"), axis=0, tiled=True),
        lax.all_gather(ln2_gain, ("fsdp", "ctx"), axis=0, tiled=True),
        lax.all_gather(ln2_bias, ("fsdp", "ctx"), axis=0, tiled=True),
    )
    qkv_full, dense_full, up_full, down_full = (gathered[0], gathered[1], gathered[2], gathered[3])
    dense_shift = gathered[4].astype(jnp.float32)
    down_shift = gathered[5].astype(jnp.float32)
    gain_one = gathered[6].astype(jnp.float32)
    shift_one = gathered[7].astype(jnp.float32)
    gain_two = gathered[8].astype(jnp.float32)
    shift_two = gathered[9].astype(jnp.float32)
    p_rows = x_prompt.shape[1]
    cont_count = x_cont.shape[1]
    cont_len = x_cont.shape[2]
    model_width = x_prompt.shape[2]
    row_count = p_rows + cont_count * cont_len
    prompt_len = p_rows * lax.axis_size("ctx")
    local_cols = qkv_full.shape[2]
    head_count = local_cols // HD
    piece_index = lax.axis_index("ctx")
    inputs = jnp.concatenate(
        [x_prompt[0], x_cont[0].reshape(cont_count * cont_len, model_width)], axis=0
    ).astype(jnp.float32)
    offsets = jnp.arange(cont_len, dtype=jnp.int32)
    prompt_pos = piece_index * p_rows + jnp.arange(p_rows, dtype=jnp.int32)
    starts = cont_start[0]
    cont_pos = (starts[:, None] + offsets[None, :]).reshape(cont_count * cont_len)
    positions = jnp.concatenate([prompt_pos, cont_pos])
    key_limit = jnp.concatenate([prompt_pos + 1, jnp.repeat(starts, cont_len)])
    own_slot = jnp.repeat(jnp.arange(cont_count, dtype=jnp.int32), cont_len)
    own_offs = jnp.tile(offsets, cont_count)
    query_slot = jnp.concatenate([jnp.full((p_rows,), -1, jnp.int32), own_slot])
    query_offs = jnp.concatenate([jnp.zeros((p_rows,), jnp.int32), own_offs])
    key_slot = jnp.concatenate([jnp.full((prompt_len,), -1, jnp.int32), own_slot])
    key_offs = jnp.concatenate([jnp.zeros((prompt_len,), jnp.int32), own_offs])
    cos_t, sin_t = rotary_tables(positions)
    cos_t = cos_t[:, None, :]
    sin_t = sin_t[:, None, :]
    row_mean = jnp.mean(inputs, axis=-1, keepdims=True)
    centered = inputs - row_mean
    scale = lax.rsqrt(jnp.mean(centered * centered, axis=-1, keepdims=True) + EPS)
    unit = centered * scale
    norm_one = unit * gain_one + shift_one
    norm_two = unit * gain_two + shift_two
    unit_low = unit.astype(jnp.bfloat16)
    ln_one = norm_one.astype(jnp.bfloat16)
    ln_two = norm_two.astype(jnp.bfloat16)
    qkv_flat = qkv_full.reshape(model_width, 3 * local_cols)
    projected = jnp.dot(ln_one, qkv_flat, preferred_element_type=jnp.float32) + qkv_bias.reshape(
        3 * local_cols
    ).astype(jnp.float32)
    projected = projected.reshape(row_count, 3, head_count, HD)
    queries = rotate(projected[:, 0], cos_t, sin_t).astype(jnp.bfloat16)
    keys_own = rotate(projected[:, 1], cos_t, sin_t).astype(jnp.bfloat16)
    values_own = projected[:, 2].astype(jnp.bfloat16)
    prompt_keys, prompt_values = (
        lax.all_gather(keys_own[:p_rows].reshape(p_rows, local_cols), "ctx", axis=0, tiled=True),
        lax.all_gather(values_own[:p_rows].reshape(p_rows, local_cols), "ctx", axis=0, tiled=True),
    )
    all_keys = jnp.concatenate(
        [prompt_keys.reshape(prompt_len, head_count, HD), keys_own[p_rows:]], axis=0
    )
    all_values = jnp.concatenate(
        [prompt_values.reshape(prompt_len, head_count, HD), values_own[p_rows:]], axis=0
    )
    scores = masked_scores(
        queries, all_keys, key_limit, query_slot, query_offs, prompt_len, key_slot, key_offs
    )
    highest = jnp.max(scores, axis=-1, keepdims=True)
    log_total = highest + jnp.log(jnp.sum(jnp.exp(scores - highest), axis=-1, keepdims=True))
    probs_low = jnp.exp(scores - log_total).astype(jnp.bfloat16)
    attended = jnp.einsum("hqk,khd->qhd", probs_low, all_values, preferred_element_type=jnp.float32)
    attended_low = attended.reshape(row_count, local_cols).astype(jnp.bfloat16)
    attn_part = jnp.dot(attended_low, dense_full, preferred_element_type=jnp.float32)
    hidden = jnp.dot(ln_two, up_full, preferred_element_type=jnp.float32) + fc1_bias.astype(
        jnp.float32
    )
    active_low = exact_gelu(hidden).astype(jnp.bfloat16)
    mlp_part = jnp.dot(active_low, down_full, preferred_element_type=jnp.float32)
    mixed = lax.psum((attn_part + mlp_part).astype(jnp.bfloat16), "tp").astype(jnp.float32)
    output = inputs + mixed + dense_shift + down_shift
    grad_out = jnp.concatenate(
        [dy_prompt[0], dy_cont[0].reshape(cont_count * cont_len, model_width)], axis=0
    )
    grad_dense = jnp.dot(attended_low.T, grad_out, preferred_element_type=jnp.float32)
    grad_down = jnp.dot(active_low.T, grad_out, preferred_element_type=jnp.float32)
    grad_shift = jnp.sum(grad_out.astype(jnp.float32), axis=0)
    grad_attended = (
        jnp.dot(grad_out, dense_full.T, preferred_element_type=jnp.float32)
        .astype(jnp.bfloat16)
        .reshape(row_count, head_count, HD)
    )
    scores = masked_scores(
        queries, all_keys, key_limit, query_slot, query_offs, prompt_len, key_slot, key_offs
    )
    probs = jnp.exp(scores - log_total)
    probs_low = probs.astype(jnp.bfloat16)
    grad_probs = jnp.einsum(
        "qhd,khd->hqk", grad_attended, all_values, preferred_element_type=jnp.float32
    )
    inner = jnp.sum(probs * grad_probs, axis=-1, keepdims=True)
    grad_scores = (probs * (grad_probs - inner)).astype(jnp.bfloat16)
    grad_queries = (
        jnp.einsum("hqk,khd->qhd", grad_scores, all_keys, preferred_element_type=jnp.float32)
        * 0.125
    )
    grad_keys = (
        jnp.einsum("hqk,qhd->khd", grad_scores, queries, preferred_element_type=jnp.float32) * 0.125
    )
    grad_values = jnp.einsum(
        "hqk,qhd->khd", probs_low, grad_attended, preferred_element_type=jnp.float32
    )
    prompt_key_grads, prompt_value_grads = (
        lax.psum_scatter(
            grad_keys[:prompt_len].reshape(prompt_len, local_cols).astype(jnp.bfloat16),
            "ctx",
            scatter_dimension=0,
            tiled=True,
        ),
        lax.psum_scatter(
            grad_values[:prompt_len].reshape(prompt_len, local_cols).astype(jnp.bfloat16),
            "ctx",
            scatter_dimension=0,
            tiled=True,
        ),
    )
    grad_keys = jnp.concatenate(
        [
            prompt_key_grads.reshape(p_rows, head_count, HD).astype(jnp.float32),
            grad_keys[prompt_len:],
        ],
        axis=0,
    )
    grad_values = jnp.concatenate(
        [
            prompt_value_grads.reshape(p_rows, head_count, HD).astype(jnp.float32),
            grad_values[prompt_len:],
        ],
        axis=0,
    )
    grad_projected = jnp.stack(
        [rotate(grad_queries, cos_t, -sin_t), rotate(grad_keys, cos_t, -sin_t), grad_values], axis=1
    )
    grad_proj_low = grad_projected.reshape(row_count, 3 * local_cols).astype(jnp.bfloat16)
    moment_one = jnp.dot(unit_low.T, grad_proj_low, preferred_element_type=jnp.float32)
    grad_qkv_bias = jnp.sum(grad_proj_low.astype(jnp.float32), axis=0)
    grad_norm_one = jnp.dot(grad_proj_low, qkv_flat.T, preferred_element_type=jnp.float32)
    grad_active = jnp.dot(grad_out, down_full.T, preferred_element_type=jnp.float32)
    gelu_back = jax.vjp(exact_gelu, hidden)[1]
    grad_hidden_low = gelu_back(grad_active)[0].astype(jnp.bfloat16)
    moment_two = jnp.dot(unit_low.T, grad_hidden_low, preferred_element_type=jnp.float32)
    grad_up_bias = jnp.sum(grad_hidden_low.astype(jnp.float32), axis=0)
    grad_norm_two = jnp.dot(grad_hidden_low, up_full.T, preferred_element_type=jnp.float32)
    turned = (grad_norm_one * gain_one + grad_norm_two * gain_two).astype(jnp.bfloat16)
    turned = lax.psum(turned, "tp").astype(jnp.float32)
    grad_inputs = grad_out.astype(jnp.float32) + scale * (
        turned
        - jnp.mean(turned, axis=-1, keepdims=True)
        - unit * jnp.mean(turned * unit, axis=-1, keepdims=True)
    )
    both = ("fsdp", "ctx")

    def scatter(array, axis):
        return lax.psum_scatter(
            array.astype(jnp.bfloat16), both, scatter_dimension=axis, tiled=True
        ).astype(jnp.float32)

    own_one = scatter(moment_one, 0)
    own_two = scatter(moment_two, 0)
    d_dense = scatter(grad_dense, 1)
    d_down = scatter(grad_down, 1)
    bias_qkv_total, bias_up_total, shift_total = lax.psum(
        (grad_qkv_bias, grad_up_bias, grad_shift), both
    )
    own_rows = w_qkv.shape[0]
    own_place = (lax.axis_index("fsdp") * lax.axis_size("ctx") + piece_index) * own_rows
    d_shift = lax.dynamic_slice_in_dim(shift_total, own_place, own_rows)
    own_qkv = w_qkv.reshape(own_rows, 3 * local_cols).astype(jnp.float32)
    own_up = w_fc1.astype(jnp.float32)
    small = lax.psum(
        jnp.stack(
            [
                jnp.sum(own_one * own_qkv, axis=1),
                jnp.sum(own_qkv * bias_qkv_total, axis=1),
                jnp.sum(own_two * own_up, axis=1),
                jnp.sum(own_up * bias_up_total, axis=1),
            ]
        ),
        "tp",
    )
    d_qkv = (
        own_one * ln1_gain.astype(jnp.float32)[:, None]
        + ln1_bias.astype(jnp.float32)[:, None] * bias_qkv_total
    ).reshape(own_rows, 3, local_cols)
    d_up = (
        own_two * ln2_gain.astype(jnp.float32)[:, None]
        + ln2_bias.astype(jnp.float32)[:, None] * bias_up_total
    )
    y_prompt = output[:p_rows][None]
    y_cont = output[p_rows:].reshape(1, cont_count, cont_len, model_width)
    dx_prompt = grad_inputs[:p_rows][None]
    dx_cont = grad_inputs[p_rows:].reshape(1, cont_count, cont_len, model_width)
    return (
        y_prompt,
        y_cont,
        dx_prompt,
        dx_cont,
        d_qkv,
        bias_qkv_total.reshape(3, local_cols),
        d_dense,
        d_shift,
        d_up,
        bias_up_total,
        d_down,
        d_shift,
        small[0],
        small[1],
        small[2],
        small[3],
    )


def solution(mesh):
    placed = (
        P("fsdp", "ctx", None),
        P("fsdp", "ctx", None, None),
        P("fsdp", "ctx"),
        P(("fsdp", "ctx"), None, "tp"),
        P(None, "tp"),
        P("tp", ("fsdp", "ctx")),
        P(("fsdp", "ctx")),
        P(("fsdp", "ctx"), "tp"),
        P("tp"),
        P("tp", ("fsdp", "ctx")),
        P(("fsdp", "ctx")),
        P(("fsdp", "ctx")),
        P(("fsdp", "ctx")),
        P(("fsdp", "ctx")),
        P(("fsdp", "ctx")),
        P("fsdp", "ctx", None),
        P("fsdp", "ctx", None, None),
    )
    return jax.shard_map(
        on_device,
        mesh=mesh,
        in_specs=placed,
        out_specs=(
            P("fsdp", "ctx", None),
            P("fsdp", "ctx", None, None),
            P("fsdp", "ctx", None),
            P("fsdp", "ctx", None, None),
            P(("fsdp", "ctx"), None, "tp"),
            P(None, "tp"),
            P("tp", ("fsdp", "ctx")),
            P(("fsdp", "ctx")),
            P(("fsdp", "ctx"), "tp"),
            P("tp"),
            P("tp", ("fsdp", "ctx")),
            P(("fsdp", "ctx")),
            P(("fsdp", "ctx")),
            P(("fsdp", "ctx")),
            P(("fsdp", "ctx")),
            P(("fsdp", "ctx")),
        ),
        check_vma=False,
    )
```

profile of v0, /device:TPU:0, one launch (start us, length us, event | category | flops | bytes accessed | tf_op | source)
XLA Modules:
  0.0 632.3 jit_solution(4390822750926472987)
XLA Ops:
  14.6 14.7 %all-gather = bf16[8,1,128]{2,1,0:T(2,128)(2,1)S(1)} all-gather(bf16[1,1,128]{2,1,0:T(2,128)(2,1)S(1)} %bitcast.164), channel_id=1, replica_groups=mesh['fsdp'=2,'ctx'=4,'tp'=4] {'fsdp','ctx'}, dimensions={0}, use_global_device_ids=true | all-gather | bytes 2304 | tf_op jit(solution)/shard_map/all_gather | solution.py:73
  29.3 13.2 %all-gather.1 = bf16[8,1,128]{2,1,0:T(2,128)(2,1)S(1)} all-gather(bf16[1,1,128]{2,1,0:T(2,128)(2,1)S(1)} %bitcast.165), channel_id=1, replica_groups=mesh['fsdp'=2,'ctx'=4,'tp'=4] {'fsdp','ctx'}, dimensions={0}, use_global_device_ids=true | all-gather | bytes 2304 | tf_op jit(solution)/shard_map/all_gather | solution.py:74
  44.1 24.7 %all_gather.41 = bf16[256,1024]{1,0:T(8,128)(2,1)S(1)} all-gather(bf16[256,128]{1,0:T(8,128)(2,1)S(1)} %copy-done.30), channel_id=1, replica_groups=mesh['fsdp'=2,'ctx'=4,'tp'=4] {'fsdp','ctx'}, dimensions={1}, use_global_device_ids=true | all-gather | bytes 589824 | tf_op jit(solution)/shard_map/all_gather | solution.py:68
  68.9 13.9 %all-gather.2 = bf16[8,1,128]{2,1,0:T(2,128)(2,1)S(1)} all-gather(bf16[1,1,128]{2,1,0:T(2,128)(2,1)S(1)} %bitcast.162), channel_id=1, replica_groups=mesh['fsdp'=2,'ctx'=4,'tp'=4] {'fsdp','ctx'}, dimensions={0}, use_global_device_ids=true | all-gather | bytes 2304 | tf_op jit(solution)/shard_map/all_gather | solution.py:75
  83.9 13.2 %all-gather.3 = bf16[8,1,128]{2,1,0:T(2,128)(2,1)S(1)} all-gather(bf16[1,1,128]{2,1,0:T(2,128)(2,1)S(1)} %bitcast.163), channel_id=1, replica_groups=mesh['fsdp'=2,'ctx'=4,'tp'=4] {'fsdp','ctx'}, dimensions={0}, use_global_device_ids=true | all-gather | bytes 2304 | tf_op jit(solution)/shard_map/all_gather | solution.py:76
  108.2 13.2 %all_gather.40 = bf16[1024,256]{0,1:T(8,128)(2,1)S(1)} all-gather(bf16[256,256]{0,1:T(8,128)(2,1)S(1)} %bitcast.143), channel_id=1, replica_groups=mesh['fsdp'=2,'ctx'=4,'tp'=4] {'ctx'}, dimensions={0}, use_global_device_ids=true | all-gather | bytes 655360 | tf_op jit(solution)/shard_map/all_gather | solution.py:130
  121.4 12.8 %fusion = (f32[4,1024]{1,0:T(4,128)S(1)}, f32[4,1024,1792]{2,1,0:T(8,128)}) fusion(pred[1024,1792]{1,0:T(8,128)(4,1)S(1)} %fusion.2, bf16[1024,4,48]{0,2,1:T(8,128)(2,1)S(1)} %slice.242, bf16[1024,4,16]{0,2,1:T(8,128)(2,1)S(1)} %get-tuple-element.95, bf16[1024,4,64]{0,2,1:T(8,128)(2,1)S(1)} %bitcast.121, bf16[1024,4,48]{0,2,1:T(8,128)(2,1)S(1)} %slice.243, ...), kind=kOutput, calls=%fused_computation.5 | convolution fusion | flops 966717440 | bytes 32784384 | tf_op jit(solution)/shard_map/qhd,khd->hqk/dot_general | solution.py:37
  134.2 13.8 %exponential_reduce_fusion = f32[4,1024]{1,0:T(4,128)S(1)} fusion(f32[4,1024,1792]{2,1,0:T(8,128)} %get-tuple-element.107, f32[4,1024]{1,0:T(4,128)S(1)} %get-tuple-element.106, pred[1024,1792]{1,0:T(8,128)(4,1)S(1)} %fusion.2), kind=kLoop, calls=%fused_computation.3 | loop fusion | flops 29356032 | bytes 31227904 | tf_op jit(solution)/shard_map/reduce_sum | solution.py:143
  148.0 12.0 %all_gather.39 = bf16[1024,256]{0,1:T(8,128)(2,1)S(1)} all-gather(bf16[256,256]{0,1:T(8,128)(2,1)S(1)} %bitcast.144), channel_id=1, replica_groups=mesh['fsdp'=2,'ctx'=4,'tp'=4] {'ctx'}, dimensions={0}, use_global_device_ids=true | all-gather | bytes 655360 | tf_op jit(solution)/shard_map/all_gather | solution.py:131
  160.1 22.0 %multiply_reduce_fusion = (f32[4,1024]{1,0:T(4,128)S(1)}, f32[4,1024,1792]{2,1,0:T(8,128)}) fusion(f32[4,1024,1792]{2,1,0:T(8,128)} %get-tuple-element.107, f32[4,1024]{1,0:T(4,128)S(1)} %log_add_fusion, pred[1024,1792]{1,0:T(8,128)(4,1)S(1)} %fusion.2, bf16[1024,4,64]{0,2,1:T(8,128)(2,1)S(1)} %bitcast.135, bf16[768,4,64]{0,2,1:T(8,128)(2,1)S(1)} %slice_bitcast_fusion.4, ...), kind=kOutput, calls=%fused_computation.1 | convolution fusion | flops 978055168 | bytes 62029824 | tf_op jit(solution)/shard_map/qhd,khd->hqk/dot_general | solution.py:171
  182.1 24.7 %multiply_convert_fusion = bf16[4,1024,1792]{2,1,0:T(8,128)(2,1)} fusion(f32[4,1024,1792]{2,1,0:T(8,128)} %get-tuple-element.109, f32[4,1024,1792]{2,1,0:T(8,128)} %get-tuple-element.107, f32[4,1024]{1,0:T(4,128)S(1)} %get-tuple-element.108, f32[4,1024]{1,0:T(4,128)S(1)} %log_add_fusion, pred[1024,1792]{1,0:T(8,128)(4,1)S(1)} %fusion.2), kind=kLoop, calls=%fused_computation | loop fusion | flops 44040192 | bytes 75268096 | tf_op jit(solution)/shard_map/convert_element_type | solution.py:175
  206.8 7.8 %fusion.25 = f32[1792,4,64]{0,2,1:T(8,128)S(1)} fusion(bf16[4,1024,1792]{2,1,0:T(8,128)(2,1)} %multiply_convert_fusion, bf16[1024,4,48]{0,2,1:T(8,128)(2,1)S(1)} %slice.243, bf16[1024,4,16]{0,2,1:T(8,128)(2,1)S(1)} %get-tuple-element.96), kind=kOutput, calls=%fused_computation.57 | convolution fusion | flops 941031424 | bytes 17039360 | tf_op jit(solution)/shard_map/hqk,qhd->khd/dot_general | solution.py:181
  216.4 14.1 %convolution_convert_fusion.3 = bf16[4,64,1024]{2,1,0:T(8,128)(2,1)} fusion(bf16[768,4,64]{0,2,1:T(8,128)(2,1)} %copy-done.13, bf16[1024,4,64]{0,2,1:T(8,128)(2,1)} %bitcast.120, f32[4,1024,1792]{2,1,0:T(8,128)} %get-tuple-element.107, f32[4,1024]{1,0:T(4,128)S(1)} %log_add_fusion, pred[1024,1792]{1,0:T(8,128)(4,1)S(1)} %fusion.2), kind=kOutput, calls=%fused_computation.83 | convolution fusion | flops 970981376 | bytes 32653312 | tf_op jit(solution)/shard_map/hqk,khd->qhd/dot_general | solution.py:145
  230.8 13.7 %convolution_bitcast_fusion = bf16[1792,4,64]{0,2,1:T(8,128)(2,1)S(1)} fusion(bf16[1024,4,64]{0,2,1:T(8,128)(2,1)} %bitcast.134, f32[4,1024,1792]{2,1,0:T(8,128)} %get-tuple-element.107, f32[4,1024]{1,0:T(4,128)S(1)} %log_add_fusion, pred[1024,1792]{1,0:T(8,128)(4,1)S(1)} %fusion.2), kind=kOutput, calls=%fused_computation.56 | convolution fusion | flops 968884224 | bytes 32653312 | tf_op jit(solution)/shard_map/hqk,qhd->khd/dot_general | solution.py:183
  246.2 10.2 %fusion.43 = f32[1024,4,64]{0,2,1:T(8,128)S(1)} fusion(bf16[4,1024,1792]{2,1,0:T(8,128)(2,1)} %multiply_convert_fusion, bf16[1024,4,48]{0,2,1:T(8,128)(2,1)} %copy-done.6, bf16[1024,4,16]{0,2,1:T(8,128)(2,1)S(1)} %get-tuple-element.95, bf16[1024,4,64]{0,2,1:T(8,128)(2,1)} %bitcast.122), kind=kOutput, calls=%fused_computation.82 | convolution fusion | flops 943915008 | bytes 16777216 | tf_op jit(solution)/shard_map/hqk,khd->qhd/dot_general | solution.py:177
  263.6 16.0 %multiply_convert_fusion.1 = (bf16[1024,1024]{1,0:T(8,128)(2,1)S(1)}, f32[1024,1024]{1,0:T(8,128)}, f32[1024,1024]{1,0:T(8,128)}) fusion(f32[1024]{0:T(1024)S(1)} %copy-done.37, bf16[1024,1024]{1,0:T(8,128)(2,1)} %all-gather.12.cloned.1.call-done, f32[1024]{0:T(1024)S(1)} %bitcast.155, f32[1024]{0:T(1024)S(1)} %bitcast.153, f32[1024]{0:T(1024)S(1)} %copy-done.34, ...), kind=kOutput, calls=%fused_computation.39 | convolution fusion | flops 2226126848 | bytes 14700544 | tf_op jit(solution)/shard_map/dot_general | solution.py:148
  280.9 3.8 convolution_convert_fusion
  284.7 3.9 copy.47
  289.2 4.7 fusion.80
  296.9 5.2 convert_reduce_fusion.3
  308.7 3.8 add_convert_fusion
  312.7 5.8 convolution_convert_fusion.1
  318.6 12.5 %all-gather.4 = bf16[8,1,128]{2,1,0:T(2,128)(2,1)S(1)} all-gather(bf16[1,1,128]{2,1,0:T(2,128)(2,1)S(1)} %bitcast.166), channel_id=1, replica_groups=mesh['fsdp'=2,'ctx'=4,'tp'=4] {'fsdp','ctx'}, dimensions={0}, use_global_device_ids=true | all-gather | bytes 2304 | tf_op jit(solution)/shard_map/all_gather | solution.py:71
  331.1 13.4 %all-gather.5 = bf16[8,1,128]{2,1,0:T(2,128)(2,1)S(1)} all-gather(bf16[1,1,128]{2,1,0:T(2,128)(2,1)S(1)} %bitcast.167), channel_id=1, replica_groups=mesh['fsdp'=2,'ctx'=4,'tp'=4] {'fsdp','ctx'}, dimensions={0}, use_global_device_ids=true | all-gather | bytes 2304 | tf_op jit(solution)/shard_map/all_gather | solution.py:72
  346.4 4.8 convolution_convert_fusion.2
  351.2 14.9 %reduce-scatter.21.cloned.1.call-done = bf16[128,1024]{1,0:T(8,128)(2,1)} async-done(((bf16[1024,1024]{1,0:T(8,128)(2,1)}), bf16[128,1024]{1,0:T(8,128)(2,1)}) %reduce-scatter.21.cloned.1.call-update) | async-done | bytes 262160
  368.1 156.4 %all-reduce.8.cloned.1.call-done = (bf16[1024,1024]{1,0:T(8,128)(2,1)}, bf16[1024,1024]{1,0:T(8,128)(2,1)}) async-done(((bf16[1024,1024]{1,0:T(8,128)(2,1)}, bf16[1024,1024]{1,0:T(8,128)(2,1)}), (bf16[1024,1024]{1,0:T(8,128)(2,1)}, bf16[1024,1024]{1,0:T(8,128)(2,1)})) %all-reduce.8.cloned.1.call-update) | async-done | bytes 4194320 | tf_op jit(solution)/shard_map/psum | solution.py:153
  528.2 6.2 convert_reduce_fusion.2
  534.4 26.8 %all-reduce.4 = (f32[768]{0:T(1024)S(1)}, f32[1024]{0:T(1024)S(1)}, f32[1024]{0:T(1024)S(1)}) all-reduce(f32[768]{0:T(1024)S(1)} %reduce_sum.126, f32[1024]{0:T(1024)S(1)} %get-tuple-element.79, f32[1024]{0:T(1024)S(1)} %get-tuple-element.110), channel_id=1, replica_groups=mesh['fsdp'=2,'ctx'=4,'tp'=4] {'fsdp','ctx'}, use_global_device_ids=true, to_apply=%region_13.14 | all-reduce | flops 2816 | bytes 22528 | tf_op jit(solution)/shard_map/psum | solution.py:245
  561.3 4.3 slice.170
  575.3 35.0 %reduce-scatter.15.cloned.1.call-done = bf16[128,768]{1,0:T(8,128)(2,1)} async-done(((bf16[1024,768]{1,0:T(8,128)(2,1)}), bf16[128,768]{1,0:T(8,128)(2,1)}) %reduce-scatter.15.cloned.1.call-update) | async-done | bytes 196624 | tf_op jit(solution)/shard_map/reduce_scatter | solution.py:237
  611.4 11.7 %psum.47 = f32[4,128]{1,0:T(4,128)S(1)} all-reduce(f32[4,128]{1,0:T(4,128)S(1)} %pad_maximum_fusion.11), channel_id=1, replica_groups=mesh['fsdp'=2,'ctx'=4,'tp'=4] {'tp'}, use_global_device_ids=true, to_apply=%region_25.26 | all-reduce | flops 512 | bytes 4096 | tf_op jit(solution)/shard_map/psum | solution.py:253
  (243 shorter events, 63.8 us)
Async XLA Ops:
  7.2 22.1 %copy-start.52 = (bf16[128]{0:T(256)(128)(2,1)S(1)}, bf16[128]{0:T(256)(128)(2,1)}, u32[]{:S(2)}) copy-start(bf16[128]{0:T(256)(128)(2,1)} %param.29) | copy-start | bytes 772
  7.2 35.3 %copy-start.43 = (bf16[3,256]{1,0:T(4,128)(2,1)S(1)}, bf16[3,256]{1,0:T(4,128)(2,1)}, u32[]{:S(2)}) copy-start(bf16[3,256]{1,0:T(4,128)(2,1)} %param.21) | copy-start | bytes 4612
  7.2 35.3 %copy-start.45 = (s32[1,3]{1,0:T(1,128)S(1)}, s32[1,3]{1,0:T(1,128)}, u32[]{:S(2)}) copy-start(s32[1,3]{1,0:T(1,128)} %param.19) | copy-start | bytes 40
  7.2 36.9 %copy-start.30 = (bf16[256,128]{1,0:T(8,128)(2,1)S(1)}, bf16[256,128]{1,0:T(8,128)(2,1)}, u32[]{:S(2)}) copy-start(bf16[256,128]{1,0:T(8,128)(2,1)} %param.22) | copy-start | bytes 196612
  7.2 61.6 %copy-start.46 = (bf16[128]{0:T(256)(128)(2,1)S(1)}, bf16[128]{0:T(256)(128)(2,1)}, u32[]{:S(2)}) copy-start(bf16[128]{0:T(256)(128)(2,1)} %param.30) | copy-start | bytes 772
  7.3 76.0 %copy-start.44 = (bf16[1024]{0:T(1024)(128)(2,1)S(1)}, bf16[1024]{0:T(1024)(128)(2,1)}, u32[]{:S(2)}) copy-start(bf16[1024]{0:T(1024)(128)(2,1)} %param.25) | copy-start | bytes 6148
  7.3 76.6 %copy-start.48 = (bf16[128]{0:T(256)(128)(2,1)S(1)}, bf16[128]{0:T(256)(128)(2,1)}, u32[]{:S(2)}) copy-start(bf16[128]{0:T(256)(128)(2,1)} %param.31) | copy-start | bytes 772
  7.3 90.5 %copy-start.14 = (bf16[1,3,256,1024]{3,2,1,0:T(8,128)(2,1)S(1)}, bf16[1,3,256,1024]{3,2,1,0:T(8,128)(2,1)}, u32[]{:S(2)}) copy-start(bf16[1,3,256,1024]{3,2,1,0:T(8,128)(2,1)} %param.33) | copy-start | bytes 4718596
  7.3 96.0 %all-gather.10.cloned.1.call-start = ((), (), s32[]{:S(2)}) async-start(), calls=%async_computation.6 | async-start | bytes 1769472 | tf_op jit(solution)/shard_map/all_gather | solution.py:67
  9.3 254.3 %all-gather.12.cloned.1.call-start = ((), (), s32[]{:S(2)}) async-start(), calls=%async_computation.7 | async-start | bytes 2359296 | tf_op jit(solution)/shard_map/all_gather | solution.py:69
  10.0 279.1 %all-gather.14.cloned.1.call-start = ((), (), s32[]{:S(2)}) async-start(), calls=%async_computation.8 | async-start | bytes 2359296 | tf_op jit(solution)/shard_map/all_gather | solution.py:70
  10.8 291.4 %reduce-scatter.11.cloned.1.call-start = ((), (), s32[]{:S(2)}) async-start(), calls=%async_computation.9 | async-start | bytes 655360 | tf_op jit(solution)/shard_map/reduce_scatter | solution.py:187
  12.8 90.5 %copy-start.31 = (f32[1024]{0:T(1024)}, f32[1024]{0:T(1024)S(1)}, u32[]{:S(2)}) copy-start(f32[1024]{0:T(1024)S(1)} %broadcast_multiply_fusion.2) | copy-start | bytes 12292
  14.6 88.8 %copy-start.33 = (f32[1024]{0:T(1024)}, f32[1024]{0:T(1024)S(1)}, u32[]{:S(2)}) copy-start(f32[1024]{0:T(1024)S(1)} %add_rsqrt_fusion) | copy-start | bytes 12292
  29.3 74.1 %copy-start.38 = (f32[8,1,128]{2,1,0:T(1,128)}, f32[8,1,128]{2,1,0:T(1,128)S(1)}, u32[]{:S(2)}) copy-start(f32[8,1,128]{2,1,0:T(1,128)S(1)} %convert_element_type.249) | copy-start | bytes 12292
  68.9 28.9 %copy-start.9 = (bf16[256,1024]{1,0:T(8,128)(2,1)}, bf16[256,1024]{1,0:T(8,128)(2,1)S(1)}, u32[]{:S(2)}) copy-start(bf16[256,1024]{1,0:T(8,128)(2,1)S(1)} %all_gather.41) | copy-start | bytes 1572868
  107.3 14.1 %copy-start.6 = (bf16[1024,4,48]{0,2,1:T(8,128)(2,1)}, bf16[1024,4,48]{0,2,1:T(8,128)(2,1)S(1)}, u32[]{:S(2)}) copy-start(bf16[1024,4,48]{0,2,1:T(8,128)(2,1)S(1)} %slice.242) | copy-start | bytes 1179652
  107.7 52.4 %copy-start.13 = (bf16[768,4,64]{0,2,1:T(8,128)(2,1)}, bf16[768,4,64]{0,2,1:T(8,128)(2,1)S(1)}, u32[]{:S(2)}) copy-start(bf16[768,4,64]{0,2,1:T(8,128)(2,1)S(1)} %slice_bitcast_fusion.4) | copy-start | bytes 1179652
  121.4 12.9 %copy-start.12 = (bf16[1024,256]{0,1:T(8,128)(2,1)}, bf16[1024,256]{0,1:T(8,128)(2,1)S(1)}, u32[]{:S(2)}) copy-start(bf16[1024,256]{0,1:T(8,128)(2,1)S(1)} %all_gather.40) | copy-start | bytes 1572868
  134.2 25.9 %copy-start.23 = (bf16[1024,256]{0,1:T(8,128)(2,1)S(1)}, bf16[1024,256]{0,1:T(8,128)(2,1)}, u32[]{:S(2)}) copy-start(bf16[1024,256]{0,1:T(8,128)(2,1)} %convolution_convert_fusion.5) | copy-start | bytes 1572868
  160.1 22.1 %copy-start.8 = (bf16[1024,256]{0,1:T(8,128)(2,1)}, bf16[1024,256]{0,1:T(8,128)(2,1)S(1)}, u32[]{:S(2)}) copy-start(bf16[1024,256]{0,1:T(8,128)(2,1)S(1)} %all_gather.39) | copy-start | bytes 1572868
  230.6 73.8 %reduce-scatter.13.cloned.1.call-start = ((), (), s32[]{:S(2)}) async-start(), calls=%async_computation.10 | async-start | bytes 655360 | tf_op jit(solution)/shard_map/reduce_scatter | solution.py:193
  246.2 12.1 %copy-start.24 = (bf16[4,64,1024]{2,1,0:T(8,128)(2,1)S(1)}, bf16[4,64,1024]{2,1,0:T(8,128)(2,1)}, u32[]{:S(2)}) copy-start(bf16[4,64,1024]{2,1,0:T(8,128)(2,1)} %convolution_convert_fusion.3) | copy-start | bytes 1572868
  246.2 12.1 %copy-start.25 = (bf16[1,256,1024]{2,1,0:T(8,128)(2,1)S(1)}, bf16[1,256,1024]{2,1,0:T(8,128)(2,1)}, u32[]{:S(2)}) copy-start(bf16[1,256,1024]{2,1,0:T(8,128)(2,1)} %param.32) | copy-start | bytes 1572868
  246.2 98.5 %reduce-scatter.19.cloned.1.call-start = ((), (), s32[]{:S(2)}) async-start(), calls=%async_computation.13 | async-start | bytes 589824
  263.5 102.6 %reduce-scatter.21.cloned.1.call-start = ((), (), s32[]{:S(2)}) async-start(), calls=%async_computation.14 | async-start | bytes 2359296
  263.6 17.3 %copy-start.16 = (bf16[1,3,256,1024]{3,2,1,0:T(8,128)(2,1)S(1)}, bf16[1,3,256,1024]{3,2,1,0:T(8,128)(2,1)}, u32[]{:S(2)}) copy-start(bf16[1,3,256,1024]{3,2,1,0:T(8,128)(2,1)} %param.33) | copy-start | bytes 4718596
  288.7 235.8 %all-reduce.8.cloned.1.call-start = ((), (), s32[]{:S(2)}) async-start(), calls=%async_computation.15 | async-start | bytes 8388608 | tf_op jit(solution)/shard_map/psum | solution.py:153
  312.6 18.5 %copy-start.55 = (bf16[128]{0:T(256)(128)(2,1)S(1)}, bf16[128]{0:T(256)(128)(2,1)}, u32[]{:S(2)}) copy-start(bf16[128]{0:T(256)(128)(2,1)} %param.27) | copy-start | bytes 772
  312.6 31.9 %copy-start.7 = (bf16[128,3,256]{0,2,1:T(8,128)(2,1)S(1)}, bf16[128,3,256]{0,2,1:T(8,128)(2,1)}, u32[]{:S(2)}) copy-start(bf16[128,3,256]{0,2,1:T(8,128)(2,1)} %copy.40) | copy-start | bytes 589828
  312.6 256.1 %reduce-scatter.17.cloned.1.call-start = ((), (), s32[]{:S(2)}) async-start(), calls=%async_computation.12 | async-start | bytes 2359296 | tf_op jit(solution)/shard_map/reduce_scatter | solution.py:237
  318.5 291.8 %reduce-scatter.15.cloned.1.call-start = ((), (), s32[]{:S(2)}) async-start(), calls=%async_computation.11 | async-start | bytes 1769472 | tf_op jit(solution)/shard_map/reduce_scatter | solution.py:237
  (42 other events, 190.8 us)
Sparse Core Ops, SparseCore 0:
  10.0 28.5 all-gather.9
  40.5 32.9 all-gather.11
  75.4 27.9 all-gather.13
  230.7 25.1 reduce-scatter.10
  259.4 24.7 reduce-scatter.12
  287.1 34.0 reduce-scatter.18
  324.9 41.2 reduce-scatter.20
  369.1 155.3 all-reduce.7
  528.1 40.5 reduce-scatter.16
  571.8 38.4 reduce-scatter.14
where the time goes:
time: 641 us; the launch traced here: 632 us
  waiting for transfers between devices  209 us (33%)
  blocking collectives  169 us (26%)
  matrix products  136 us (21%)
  other arithmetic  68.7 us (11%)
  local copies, waits for them, and re-layouts  32.7 us (5%)
  between operations  15.3 us (2%)
    psum x1, waiting for transfers between devices, on_device(): lax.psum((attn_part + mlp_part).astype(jnp.bfloat16), 'tp')  156 us
    reduce_scatter x2, waiting for transfers between devices, scatter(): lax.psum_scatter(array.astype(jnp.bfloat16), both, scatter_dimension=axis...  36 us
    psum x1, blocking collectives, on_device(): lax.psum((grad_qkv_bias, grad_up_bias, grad_shift), both)  26.8 us
    all_gather x1, blocking collectives, on_device(): lax.all_gather(w_dense, ('fsdp', 'ctx'), axis=1, tiled=True)  24.7 us
    convert_element_type x1, other arithmetic, on_device(): grad_scores = (probs * (grad_probs - inner)).astype(jnp.bfloat16)  24.7 us
    dot_general x1, matrix products, on_device(): jnp.einsum('qhd,khd->hqk', grad_attended, all_values, preferred_element_t...  22 us
    unnamed x12, waiting for transfers between devices  16.4 us
    unnamed x135, local copies, waits for them, and re-layouts  16.1 us
  transfers between devices with their start and end apart: 10, of which 4 were waited for; matrix products, arithmetic and copies ran while one was open for 36% of the time, Pallas kernels for 0%

commit v1 on v0

--- a/solution.py
+++ b/solution.py
@@ -6,6 +6,18 @@
 HD = 64
 ROT = 16
 EPS = 1e-05
+
+
+def gather_by_bits(x, axis, dim):
+    ways, here, turn = (lax.axis_size(axis), lax.axis_index(axis), x.shape[dim])
+    line, have = (x, 1)
+    while have < ways:
+        line = jnp.concatenate(
+            [line, lax.ppermute(line, axis, [(d, (d - have) % ways) for d in range(ways)])],
+            axis=dim,
+        )
+        have = 2 * have
+    return jnp.roll(line, here * turn, axis=dim)
 
 
 def exact_gelu(values):
@@ -72,7 +84,7 @@
         lax.all_gather(fc2_bias, ("fsdp", "ctx"), axis=0, tiled=True),
         lax.all_gather(ln1_gain, ("fsdp", "ctx"), axis=0, tiled=True),
         lax.all_gather(ln1_bias, ("fsdp", "ctx"), axis=0, tiled=True),
-        lax.all_gather(ln2_gain, ("fsdp", "ctx"), axis=0, tiled=True),
+        gather_by_bits(ln2_gain, ("fsdp", "ctx"), 0),
         lax.all_gather(ln2_bias, ("fsdp", "ctx"), axis=0, tiled=True),
     )
     qkv_full, dense_full, up_full, down_full = (gathered[0], gathered[1], gathered[2], gathered[3])

time: 641 us -> 632 us (0.986)
  blocking collectives: 169 us -> 152 us
    all_gather x1 -> x0, blocking collectives: 13.9 us -> none  [on_device(): lax.all_gather(ln2_gain, ('fsdp', 'ctx'), axis=0, tiled=True)]
    unnamed x135 -> x142, local copies, waits for them, and re-layouts: 16.1 us -> 18.4 us
  transfers between devices with their start and end apart: 10 -> 13, of which waited for: 4 -> 5; matrix products, arithmetic and copies ran while one was open for 36% -> 37% of each run, Pallas kernels for 0% -> 0%
where the time goes in v1:
time: 632 us; the launch traced here: 624 us
  waiting for transfers between devices  210 us (33%)
  blocking collectives  152 us (24%)
  matrix products  136 us (22%)
  other arithmetic  68.8 us (11%)
  local copies, waits for them, and re-layouts  35.1 us (6%)
  between operations  15.4 us (2%)
  starting transfers between devices  6.94 us (1%)
    psum x1, waiting for transfers between devices, on_device(): lax.psum((attn_part + mlp_part).astype(jnp.bfloat16), 'tp')  156 us
    reduce_scatter x2, waiting for transfers between devices, scatter(): lax.psum_scatter(array.astype(jnp.bfloat16), both, scatter_dimension=axis...  36.1 us
    psum x1, blocking collectives, on_device(): lax.psum((grad_qkv_bias, grad_up_bias, grad_shift), both)  26.9 us
    convert_element_type x1, other arithmetic, on_device(): grad_scores = (probs * (grad_probs - inner)).astype(jnp.bfloat16)  24.7 us
    all_gather x1, blocking collectives, on_device(): lax.all_gather(w_dense, ('fsdp', 'ctx'), axis=1, tiled=True)  24.2 us
    dot_general x1, matrix products, on_device(): jnp.einsum('qhd,khd->hqk', grad_attended, all_values, preferred_element_t...  22 us
    unnamed x142, local copies, waits for them, and re-layouts  18.4 us
    unnamed x12, waiting for transfers between devices  16.1 us
  transfers between devices with their start and end apart: 13, of which 5 were waited for; matrix products, arithmetic and copies ran while one was open for 37% of the time, Pallas kernels for 0%

profile of v1, /device:TPU:0, one launch (start us, length us, event | category | flops | bytes accessed | tf_op | source)
XLA Modules:
  0.0 624.4 jit_solution(5250205102601865236)
XLA Ops:
  17.3 12.0 %all-gather = bf16[8,1,128]{2,1,0:T(2,128)(2,1)S(1)} all-gather(bf16[1,1,128]{2,1,0:T(2,128)(2,1)S(1)} %bitcast.159), channel_id=1, replica_groups=mesh['fsdp'=2,'ctx'=4,'tp'=4] {'fsdp','ctx'}, dimensions={0}, use_global_device_ids=true | all-gather | bytes 2304 | tf_op jit(solution)/shard_map/all_gather | solution.py:85
  29.3 13.9 %all-gather.1 = bf16[8,1,128]{2,1,0:T(2,128)(2,1)S(1)} all-gather(bf16[1,1,128]{2,1,0:T(2,128)(2,1)S(1)} %bitcast.160), channel_id=1, replica_groups=mesh['fsdp'=2,'ctx'=4,'tp'=4] {'fsdp','ctx'}, dimensions={0}, use_global_device_ids=true | all-gather | bytes 2304 | tf_op jit(solution)/shard_map/all_gather | solution.py:86
  44.8 24.2 %all_gather.38 = bf16[256,1024]{1,0:T(8,128)(2,1)S(1)} all-gather(bf16[256,128]{1,0:T(8,128)(2,1)S(1)} %copy-done.30), channel_id=1, replica_groups=mesh['fsdp'=2,'ctx'=4,'tp'=4] {'fsdp','ctx'}, dimensions={1}, use_global_device_ids=true | all-gather | bytes 589824 | tf_op jit(solution)/shard_map/all_gather | solution.py:80
  79.6 12.9 %all-gather.2 = bf16[8,1,128]{2,1,0:T(2,128)(2,1)S(1)} all-gather(bf16[1,1,128]{2,1,0:T(2,128)(2,1)S(1)} %bitcast.158), channel_id=1, replica_groups=mesh['fsdp'=2,'ctx'=4,'tp'=4] {'fsdp','ctx'}, dimensions={0}, use_global_device_ids=true | all-gather | bytes 2304 | tf_op jit(solution)/shard_map/all_gather | solution.py:88
  100.3 13.1 %all_gather.37 = bf16[1024,256]{0,1:T(8,128)(2,1)S(1)} all-gather(bf16[256,256]{0,1:T(8,128)(2,1)S(1)} %bitcast.141), channel_id=1, replica_groups=mesh['fsdp'=2,'ctx'=4,'tp'=4] {'ctx'}, dimensions={0}, use_global_device_ids=true | all-gather | bytes 655360 | tf_op jit(solution)/shard_map/all_gather | solution.py:142
  113.4 12.8 %fusion = (f32[4,1024]{1,0:T(4,128)S(1)}, f32[4,1024,1792]{2,1,0:T(8,128)}) fusion(pred[1024,1792]{1,0:T(8,128)(4,1)S(1)} %fusion.2, bf16[1024,4,48]{0,2,1:T(8,128)(2,1)S(1)} %slice.242, bf16[1024,4,16]{0,2,1:T(8,128)(2,1)S(1)} %get-tuple-element.95, bf16[1024,4,64]{0,2,1:T(8,128)(2,1)S(1)} %bitcast.119, bf16[1024,4,48]{0,2,1:T(8,128)(2,1)S(1)} %slice.243, ...), kind=kOutput, calls=%fused_computation.5 | convolution fusion | flops 966717440 | bytes 32784384 | tf_op jit(solution)/shard_map/qhd,khd->hqk/dot_general | solution.py:49
  126.2 13.8 %exponential_reduce_fusion = f32[4,1024]{1,0:T(4,128)S(1)} fusion(f32[4,1024,1792]{2,1,0:T(8,128)} %get-tuple-element.107, f32[4,1024]{1,0:T(4,128)S(1)} %get-tuple-element.106, pred[1024,1792]{1,0:T(8,128)(4,1)S(1)} %fusion.2), kind=kLoop, calls=%fused_computation.3 | loop fusion | flops 29356032 | bytes 31227904 | tf_op jit(solution)/shard_map/reduce_sum | solution.py:155
  140.1 12.0 %all_gather.36 = bf16[1024,256]{0,1:T(8,128)(2,1)S(1)} all-gather(bf16[256,256]{0,1:T(8,128)(2,1)S(1)} %bitcast.142), channel_id=1, replica_groups=mesh['fsdp'=2,'ctx'=4,'tp'=4] {'ctx'}, dimensions={0}, use_global_device_ids=true | all-gather | bytes 655360 | tf_op jit(solution)/shard_map/all_gather | solution.py:143
  152.1 22.0 %multiply_reduce_fusion = (f32[4,1024]{1,0:T(4,128)S(1)}, f32[4,1024,1792]{2,1,0:T(8,128)}) fusion(f32[4,1024,1792]{2,1,0:T(8,128)} %get-tuple-element.107, f32[4,1024]{1,0:T(4,128)S(1)} %log_add_fusion, pred[1024,1792]{1,0:T(8,128)(4,1)S(1)} %fusion.2, bf16[1024,4,64]{0,2,1:T(8,128)(2,1)S(1)} %bitcast.133, bf16[768,4,64]{0,2,1:T(8,128)(2,1)S(1)} %slice_bitcast_fusion.4, ...), kind=kOutput, calls=%fused_computation.1 | convolution fusion | flops 978055168 | bytes 62029824 | tf_op jit(solution)/shard_map/qhd,khd->hqk/dot_general | solution.py:183
  174.1 24.7 %multiply_convert_fusion = bf16[4,1024,1792]{2,1,0:T(8,128)(2,1)} fusion(f32[4,1024,1792]{2,1,0:T(8,128)} %get-tuple-element.109, f32[4,1024,1792]{2,1,0:T(8,128)} %get-tuple-element.107, f32[4,1024]{1,0:T(4,128)S(1)} %get-tuple-element.108, f32[4,1024]{1,0:T(4,128)S(1)} %log_add_fusion, pred[1024,1792]{1,0:T(8,128)(4,1)S(1)} %fusion.2), kind=kLoop, calls=%fused_computation | loop fusion | flops 44040192 | bytes 75268096 | tf_op jit(solution)/shard_map/convert_element_type | solution.py:187
  198.7 7.8 %fusion.25 = f32[1792,4,64]{0,2,1:T(8,128)S(1)} fusion(bf16[4,1024,1792]{2,1,0:T(8,128)(2,1)} %multiply_convert_fusion, bf16[1024,4,48]{0,2,1:T(8,128)(2,1)S(1)} %slice.243, bf16[1024,4,16]{0,2,1:T(8,128)(2,1)S(1)} %get-tuple-element.96), kind=kOutput, calls=%fused_computation.57 | convolution fusion | flops 941031424 | bytes 17039360 | tf_op jit(solution)/shard_map/hqk,qhd->khd/dot_general | solution.py:193
  208.4 14.1 %convolution_convert_fusion.3 = bf16[4,64,1024]{2,1,0:T(8,128)(2,1)} fusion(bf16[768,4,64]{0,2,1:T(8,128)(2,1)} %copy-done.13, bf16[1024,4,64]{0,2,1:T(8,128)(2,1)} %bitcast.118, f32[4,1024,1792]{2,1,0:T(8,128)} %get-tuple-element.107, f32[4,1024]{1,0:T(4,128)S(1)} %log_add_fusion, pred[1024,1792]{1,0:T(8,128)(4,1)S(1)} %fusion.2), kind=kOutput, calls=%fused_computation.83 | convolution fusion | flops 970981376 | bytes 32653312 | tf_op jit(solution)/shard_map/hqk,khd->qhd/dot_general | solution.py:157
  223.0 13.7 %convolution_bitcast_fusion = bf16[1792,4,64]{0,2,1:T(8,128)(2,1)S(1)} fusion(bf16[1024,4,64]{0,2,1:T(8,128)(2,1)} %bitcast.132, f32[4,1024,1792]{2,1,0:T(8,128)} %get-tuple-element.107, f32[4,1024]{1,0:T(4,128)S(1)} %log_add_fusion, pred[1024,1792]{1,0:T(8,128)(4,1)S(1)} %fusion.2), kind=kOutput, calls=%fused_computation.56 | convolution fusion | flops 968884224 | bytes 32653312 | tf_op jit(solution)/shard_map/hqk,qhd->khd/dot_general | solution.py:195
  238.4 10.2 %fusion.43 = f32[1024,4,64]{0,2,1:T(8,128)S(1)} fusion(bf16[4,1024,1792]{2,1,0:T(8,128)(2,1)} %multiply_convert_fusion, bf16[1024,4,48]{0,2,1:T(8,128)(2,1)} %copy-done.6, bf16[1024,4,16]{0,2,1:T(8,128)(2,1)S(1)} %get-tuple-element.95, bf16[1024,4,64]{0,2,1:T(8,128)(2,1)} %bitcast.120), kind=kOutput, calls=%fused_computation.82 | convolution fusion | flops 943915008 | bytes 16777216 | tf_op jit(solution)/shard_map/hqk,khd->qhd/dot_general | solution.py:189
  255.8 15.9 %multiply_convert_fusion.1 = (bf16[1024,1024]{1,0:T(8,128)(2,1)S(1)}, f32[1024,1024]{1,0:T(8,128)}, f32[1024,1024]{1,0:T(8,128)}) fusion(f32[1024]{0:T(1024)S(1)} %copy-done.39, bf16[1024,1024]{1,0:T(8,128)(2,1)} %all-gather.11.cloned.1.call-done, f32[1024]{0:T(1024)S(1)} %bitcast.151, f32[1024]{0:T(1024)S(1)} %copy-done.43, f32[1024]{0:T(1024)S(1)} %copy-done.34, ...), kind=kOutput, calls=%fused_computation.39 | convolution fusion | flops 2226126848 | bytes 14700544 | tf_op jit(solution)/shard_map/dot_general | solution.py:160
  273.0 3.8 convolution_convert_fusion
  276.8 3.9 copy.47
  281.0 4.7 fusion.80
  288.8 5.2 convert_reduce_fusion.3
  300.6 3.8 add_convert_fusion
  304.5 5.8 convolution_convert_fusion.1
  310.5 12.3 %all-gather.3 = bf16[8,1,128]{2,1,0:T(2,128)(2,1)S(1)} all-gather(bf16[1,1,128]{2,1,0:T(2,128)(2,1)S(1)} %bitcast.161), channel_id=1, replica_groups=mesh['fsdp'=2,'ctx'=4,'tp'=4] {'fsdp','ctx'}, dimensions={0}, use_global_device_ids=true | all-gather | bytes 2304 | tf_op jit(solution)/shard_map/all_gather | solution.py:83
  322.8 13.4 %all-gather.4 = bf16[8,1,128]{2,1,0:T(2,128)(2,1)S(1)} all-gather(bf16[1,1,128]{2,1,0:T(2,128)(2,1)S(1)} %bitcast.162), channel_id=1, replica_groups=mesh['fsdp'=2,'ctx'=4,'tp'=4] {'fsdp','ctx'}, dimensions={0}, use_global_device_ids=true | all-gather | bytes 2304 | tf_op jit(solution)/shard_map/all_gather | solution.py:84
  338.1 4.8 convolution_convert_fusion.2
  342.9 15.2 %reduce-scatter.21.cloned.1.call-done = bf16[128,1024]{1,0:T(8,128)(2,1)} async-done(((bf16[1024,1024]{1,0:T(8,128)(2,1)}), bf16[128,1024]{1,0:T(8,128)(2,1)}) %reduce-scatter.21.cloned.1.call-update) | async-done | bytes 262160
  360.1 156.4 %all-reduce.8.cloned.1.call-done = (bf16[1024,1024]{1,0:T(8,128)(2,1)}, bf16[1024,1024]{1,0:T(8,128)(2,1)}) async-done(((bf16[1024,1024]{1,0:T(8,128)(2,1)}, bf16[1024,1024]{1,0:T(8,128)(2,1)}), (bf16[1024,1024]{1,0:T(8,128)(2,1)}, bf16[1024,1024]{1,0:T(8,128)(2,1)})) %all-reduce.8.cloned.1.call-update) | async-done | bytes 4194320 | tf_op jit(solution)/shard_map/psum | solution.py:165
  516.5 3.7 convert_reduce_fusion
  520.3 6.2 convert_reduce_fusion.2
  526.4 26.9 %all-reduce.4 = (f32[768]{0:T(1024)S(1)}, f32[1024]{0:T(1024)S(1)}, f32[1024]{0:T(1024)S(1)}) all-reduce(f32[768]{0:T(1024)S(1)} %reduce_sum.126, f32[1024]{0:T(1024)S(1)} %get-tuple-element.79, f32[1024]{0:T(1024)S(1)} %get-tuple-element.110), channel_id=1, replica_groups=mesh['fsdp'=2,'ctx'=4,'tp'=4] {'fsdp','ctx'}, use_global_device_ids=true, to_apply=%region_13.14 | all-reduce | flops 2816 | bytes 22528 | tf_op jit(solution)/shard_map/psum | solution.py:257
  553.3 4.3 slice.170
  567.3 35.0 %reduce-scatter.15.cloned.1.call-done = bf16[128,768]{1,0:T(8,128)(2,1)} async-done(((bf16[1024,768]{1,0:T(8,128)(2,1)}), bf16[128,768]{1,0:T(8,128)(2,1)}) %reduce-scatter.15.cloned.1.call-update) | async-done | bytes 196624 | tf_op jit(solution)/shard_map/reduce_scatter | solution.py:249
  603.4 11.7 %psum.47 = f32[4,128]{1,0:T(4,128)S(1)} all-reduce(f32[4,128]{1,0:T(4,128)S(1)} %pad_maximum_fusion.11), channel_id=1, replica_groups=mesh['fsdp'=2,'ctx'=4,'tp'=4] {'tp'}, use_global_device_ids=true, to_apply=%region_25.26 | all-reduce | flops 512 | bytes 4096 | tf_op jit(solution)/shard_map/psum | solution.py:265
  (259 shorter events, 68.8 us)
Async XLA Ops:
  7.2 22.1 %copy-start.52 = (bf16[128]{0:T(256)(128)(2,1)S(1)}, bf16[128]{0:T(256)(128)(2,1)}, u32[]{:S(2)}) copy-start(bf16[128]{0:T(256)(128)(2,1)} %param.29) | copy-start | bytes 772
  7.2 36.0 %copy-start.47 = (s32[1,3]{1,0:T(1,128)S(1)}, s32[1,3]{1,0:T(1,128)}, u32[]{:S(2)}) copy-start(s32[1,3]{1,0:T(1,128)} %param.19) | copy-start | bytes 40
  7.2 37.6 %copy-start.30 = (bf16[256,128]{1,0:T(8,128)(2,1)S(1)}, bf16[256,128]{1,0:T(8,128)(2,1)}, u32[]{:S(2)}) copy-start(bf16[256,128]{1,0:T(8,128)(2,1)} %param.22) | copy-start | bytes 196612
  7.2 62.7 %copy-start.14 = (bf16[1,3,256,1024]{3,2,1,0:T(8,128)(2,1)S(1)}, bf16[1,3,256,1024]{3,2,1,0:T(8,128)(2,1)}, u32[]{:S(2)}) copy-start(bf16[1,3,256,1024]{3,2,1,0:T(8,128)(2,1)} %param.33) | copy-start | bytes 4718596
  7.2 88.2 %all-gather.9.cloned.1.call-start = ((), (), s32[]{:S(2)}) async-start(), calls=%async_computation.6 | async-start | bytes 1769472 | tf_op jit(solution)/shard_map/all_gather | solution.py:79
  9.2 246.5 %all-gather.11.cloned.1.call-start = ((), (), s32[]{:S(2)}) async-start(), calls=%async_computation.7 | async-start | bytes 2359296 | tf_op jit(solution)/shard_map/all_gather | solution.py:81
  10.0 271.0 %all-gather.13.cloned.1.call-start = ((), (), s32[]{:S(2)}) async-start(), calls=%async_computation.8 | async-start | bytes 2359296 | tf_op jit(solution)/shard_map/all_gather | solution.py:82
  10.0 65.5 %collective-permute-start = (bf16[128]{0:T(256)(128)(2,1)}, bf16[128]{0:T(256)(128)(2,1)S(1)}, u32[]{:S(2)}, u32[]{:S(2)}) collective-permute-start(bf16[128]{0:T(256)(128)(2,1)} %param.30), channel_id=1, source_target_pairs={{0,28},{4,0},{8,4},{12,8},{16,12},{20,16},{24,20},{28,24},{1,29},{... | collective-permute-start | bytes 776 | tf_op jit(solution)/shard_map/ppermute | solution.py:16
  13.5 280.6 %reduce-scatter.11.cloned.1.call-start = ((), (), s32[]{:S(2)}) async-start(), calls=%async_computation.9 | async-start | bytes 655360 | tf_op jit(solution)/shard_map/reduce_scatter | solution.py:199
  15.5 79.9 %copy-start.31 = (f32[1024]{0:T(1024)}, f32[1024]{0:T(1024)S(1)}, u32[]{:S(2)}) copy-start(f32[1024]{0:T(1024)S(1)} %broadcast_multiply_fusion.2) | copy-start | bytes 12292
  17.3 78.2 %copy-start.33 = (f32[1024]{0:T(1024)}, f32[1024]{0:T(1024)S(1)}, u32[]{:S(2)}) copy-start(f32[1024]{0:T(1024)S(1)} %add_rsqrt_fusion) | copy-start | bytes 12292
  43.3 32.2 %copy-start.45 = (bf16[3,256]{1,0:T(4,128)(2,1)S(1)}, bf16[3,256]{1,0:T(4,128)(2,1)}, u32[]{:S(2)}) copy-start(bf16[3,256]{1,0:T(4,128)(2,1)} %param.21) | copy-start | bytes 4612
  43.3 32.3 %copy-start.36 = (bf16[128]{0:T(256)(128)(2,1)S(1)}, bf16[128]{0:T(256)(128)(2,1)}, u32[]{:S(2)}) copy-start(bf16[128]{0:T(256)(128)(2,1)} %param.30) | copy-start | bytes 772
  43.5 34.3 %copy-start.46 = (bf16[1024]{0:T(1024)(128)(2,1)S(1)}, bf16[1024]{0:T(1024)(128)(2,1)}, u32[]{:S(2)}) copy-start(bf16[1024]{0:T(1024)(128)(2,1)} %param.25) | copy-start | bytes 6148
  43.5 36.1 %copy-start.48 = (bf16[128]{0:T(256)(128)(2,1)S(1)}, bf16[128]{0:T(256)(128)(2,1)}, u32[]{:S(2)}) copy-start(bf16[128]{0:T(256)(128)(2,1)} %param.31) | copy-start | bytes 772
  75.5 23.5 %copy-start.40 = (f32[8,1,128]{2,1,0:T(1,128)}, f32[8,1,128]{2,1,0:T(1,128)S(1)}, u32[]{:S(2)}) copy-start(f32[8,1,128]{2,1,0:T(1,128)S(1)} %convert_element_type.249) | copy-start | bytes 12292
  75.6 3.7 collective-permute-start.1
  79.3 14.5 %collective-permute-start.2 = (bf16[512]{0:T(512)(128)(2,1)S(1)}, bf16[512]{0:T(512)(128)(2,1)S(1)}, u32[]{:S(2)}, u32[]{:S(2)}) collective-permute-start(bf16[512]{0:T(512)(128)(2,1)S(1)} %pad_maximum_fusion.12), channel_id=1, source_target_pairs={{0,16},{4,20},{8,24},{12,28},{16,0},{20,4},{24,8},{28,12},{1,17},{... | collective-permute-start | bytes 3080 | tf_op jit(solution)/shard_map/ppermute | solution.py:16
  99.4 14.1 %copy-start.6 = (bf16[1024,4,48]{0,2,1:T(8,128)(2,1)}, bf16[1024,4,48]{0,2,1:T(8,128)(2,1)S(1)}, u32[]{:S(2)}) copy-start(bf16[1024,4,48]{0,2,1:T(8,128)(2,1)S(1)} %slice.242) | copy-start | bytes 1179652
  99.8 52.3 %copy-start.13 = (bf16[768,4,64]{0,2,1:T(8,128)(2,1)}, bf16[768,4,64]{0,2,1:T(8,128)(2,1)S(1)}, u32[]{:S(2)}) copy-start(bf16[768,4,64]{0,2,1:T(8,128)(2,1)S(1)} %slice_bitcast_fusion.4) | copy-start | bytes 1179652
  113.4 12.8 %copy-start.12 = (bf16[1024,256]{0,1:T(8,128)(2,1)}, bf16[1024,256]{0,1:T(8,128)(2,1)S(1)}, u32[]{:S(2)}) copy-start(bf16[1024,256]{0,1:T(8,128)(2,1)S(1)} %all_gather.37) | copy-start | bytes 1572868
  126.2 25.8 %copy-start.23 = (bf16[1024,256]{0,1:T(8,128)(2,1)S(1)}, bf16[1024,256]{0,1:T(8,128)(2,1)}, u32[]{:S(2)}) copy-start(bf16[1024,256]{0,1:T(8,128)(2,1)} %convolution_convert_fusion.5) | copy-start | bytes 1572868
  152.0 22.0 %copy-start.8 = (bf16[1024,256]{0,1:T(8,128)(2,1)}, bf16[1024,256]{0,1:T(8,128)(2,1)S(1)}, u32[]{:S(2)}) copy-start(bf16[1024,256]{0,1:T(8,128)(2,1)S(1)} %all_gather.36) | copy-start | bytes 1572868
  222.5 73.7 %reduce-scatter.13.cloned.1.call-start = ((), (), s32[]{:S(2)}) async-start(), calls=%async_computation.10 | async-start | bytes 655360 | tf_op jit(solution)/shard_map/reduce_scatter | solution.py:205
  238.3 98.0 %reduce-scatter.19.cloned.1.call-start = ((), (), s32[]{:S(2)}) async-start(), calls=%async_computation.13 | async-start | bytes 589824
  255.6 102.5 %reduce-scatter.21.cloned.1.call-start = ((), (), s32[]{:S(2)}) async-start(), calls=%async_computation.14 | async-start | bytes 2359296
  255.8 17.2 %copy-start.16 = (bf16[1,3,256,1024]{3,2,1,0:T(8,128)(2,1)S(1)}, bf16[1,3,256,1024]{3,2,1,0:T(8,128)(2,1)}, u32[]{:S(2)}) copy-start(bf16[1,3,256,1024]{3,2,1,0:T(8,128)(2,1)} %param.33) | copy-start | bytes 4718596
  280.8 235.7 %all-reduce.8.cloned.1.call-start = ((), (), s32[]{:S(2)}) async-start(), calls=%async_computation.15 | async-start | bytes 8388608 | tf_op jit(solution)/shard_map/psum | solution.py:165
  304.5 18.3 %copy-start.55 = (bf16[128]{0:T(256)(128)(2,1)S(1)}, bf16[128]{0:T(256)(128)(2,1)}, u32[]{:S(2)}) copy-start(bf16[128]{0:T(256)(128)(2,1)} %param.27) | copy-start | bytes 772
  304.5 31.7 %copy-start.7 = (bf16[128,3,256]{0,2,1:T(8,128)(2,1)S(1)}, bf16[128,3,256]{0,2,1:T(8,128)(2,1)}, u32[]{:S(2)}) copy-start(bf16[128,3,256]{0,2,1:T(8,128)(2,1)} %copy.40) | copy-start | bytes 589828
  304.5 256.2 %reduce-scatter.17.cloned.1.call-start = ((), (), s32[]{:S(2)}) async-start(), calls=%async_computation.12 | async-start | bytes 2359296 | tf_op jit(solution)/shard_map/reduce_scatter | solution.py:249
  310.4 292.0 %reduce-scatter.15.cloned.1.call-start = ((), (), s32[]{:S(2)}) async-start(), calls=%async_computation.11 | async-start | bytes 1769472 | tf_op jit(solution)/shard_map/reduce_scatter | solution.py:249
  (45 other events, 221.0 us)
Sparse Core Ops, SparseCore 0:
  10.0 28.5 all-gather.8
  40.5 33.1 all-gather.10
  75.6 27.6 all-gather.12
  222.6 25.1 reduce-scatter.10
  251.4 24.7 reduce-scatter.12
  279.1 34.1 reduce-scatter.18
  316.9 41.2 reduce-scatter.20
  361.1 155.3 all-reduce.7
  520.1 40.5 reduce-scatter.16
  563.9 38.4 reduce-scatter.14
